TPU v7x, 32 devices: a whole 2x2x4 slice. The times are simulated.
32 devices in a mesh: row: 4 (over x, core), col: 8 (over z, y).
Axes of the slice: x: 2, y: 2, z: 4, core: 2. Of those that a mesh axis runs over, the one named last changes fastest.
Arguments:
- item_ids: int32 [8192], P(('row', 'col')), may hold values from 0 to 63
- user_lengths: int32 [8], replicated, may hold values from 1 to 2048, 8192 in all
- catalogue: bfloat16 [64, 1024], P(('row', 'col')), may hold values from -6 to 6
- tap_lengths: int32 [1, 1024], replicated, may hold values from 64 to 256
- conv_taps: bfloat16 [1, 256, 1024], replicated, may hold values from -0.375 to 0.375
- norm_gains: float32 [1, 2, 1024], replicated, may hold values from 0.1 to 1.9
- gate_weight: bfloat16 [1, 1024, 1024], P(None, 'col'), may hold values from -0.1875 to 0.1875
- up_weight: bfloat16 [1, 1024, 1024], P(None, 'col'), may hold values from -0.1875 to 0.1875
- down_weight: bfloat16 [1, 1024, 1024], P(None, 'col'), may hold values from -0.1875 to 0.1875
Outputs:
- history_out: bfloat16 [8192, 1024], P(('row', 'col'))
Inputs may be any that keep to these rules, and one draw needn't show every extreme that they name: `user_lengths`: the 8 lengths sum to 8192.
All inputs are finite; a program needn't handle non-finite values.
Results may differ from a plain program's by a relative error of at most 0.0054.
Values may be sent and summed in bfloat16 or wider, within the bound.
No kernel may reach another device: no remote copies, remote signals or barrier semaphores. Data moves between devices by JAX's collectives and lax.ppermute only.
A program may use at most 64 MiB of HBM per device.

v0:
```python
import jax
import jax.numpy as jnp
from jax import lax
from jax.sharding import PartitionSpec as P

epsilon = 1e-06
group_taps = 32


def from_behind(block, axis, distance):
    devices = range(lax.axis_size(axis))
    route = [(i - distance, i) for i in devices if i - distance in devices]
    return lax.ppermute(block, axis, route)


def rms_norm(values, gains):
    scale = lax.rsqrt(jnp.mean(values * values, axis=-1, keepdims=True) + epsilon)
    return values * scale * gains


def token_ages(positions, user_starts):
    reached = user_starts[None, :] <= positions[:, None]
    fallback = jnp.minimum(positions, 0)[:, None]
    seg_start = jnp.max(jnp.where(reached, user_starts[None, :], fallback), axis=1)
    return positions - seg_start


def earlier_items(item_ids, wanted):
    current = item_ids
    pieces = []
    current = from_behind(current, ("row", "col"), 1)
    pieces = [current] + pieces
    return pieces[0][-wanted:]


def convolve(extended, tap_table, token_age, out_rows):
    reach = extended.shape[0] - out_rows
    groups = -(-tap_table.shape[0] // group_taps)

    def one_group(group_index, accumulated):
        for within in range(group_taps):
            lag_index = group_index * group_taps + within
            shifted = lax.dynamic_slice_in_dim(extended, reach - lag_index, out_rows, 0)
            weights = lax.dynamic_slice_in_dim(tap_table, lag_index, 1, 0)
            keep = (lag_index <= token_age)[:, None]
            accumulated = accumulated + jnp.where(keep, shifted * weights, 0.0)
        return accumulated

    blank = jnp.zeros((out_rows, extended.shape[1]), jnp.float32)
    return lax.fori_loop(0, groups, one_group, blank)


def feed_forward(hidden, gains_row, gate_rows, up_rows, down_rows):
    inner = rms_norm(hidden, gains_row).astype(jnp.bfloat16)
    columns = inner
    first_sum = jnp.dot(
        columns,
        lax.all_gather(gate_rows, "col", axis=0, tiled=True),
        preferred_element_type=jnp.float32,
    )
    second_sum = jnp.dot(
        columns,
        lax.all_gather(up_rows, "col", axis=0, tiled=True),
        preferred_element_type=jnp.float32,
    )
    activated = (jax.nn.silu(first_sum) * second_sum).astype(jnp.bfloat16)
    columns = activated
    projected = jnp.dot(
        columns,
        lax.all_gather(down_rows, "col", axis=0, tiled=True),
        preferred_element_type=jnp.float32,
    )
    return hidden + projected


def body(
    item_ids,
    user_lengths,
    catalogue,
    tap_lengths,
    conv_taps,
    norm_gains,
    gate_weight,
    up_weight,
    down_weight,
):
    row_count = item_ids.shape[0]
    reach = conv_taps.shape[1] - 1
    layer_count = conv_taps.shape[0]
    catalogue_all = lax.all_gather(catalogue, ("row", "col"), axis=0, tiled=True)
    device_index = lax.axis_index("row") * lax.axis_size("col") + lax.axis_index("col")
    first_row = device_index * row_count
    user_starts = jnp.cumsum(user_lengths) - user_lengths
    lag_column = jnp.arange(conv_taps.shape[1], dtype=jnp.int32)[:, None]
    tap_tables = conv_taps.astype(jnp.float32) * (
        lag_column[None] < tap_lengths[:, None, :]
    ).astype(jnp.float32)
    extra = reach * layer_count
    wide_ids = jnp.concatenate([earlier_items(item_ids, extra), item_ids], axis=0)
    hidden = jnp.take(catalogue_all, wide_ids, axis=0).astype(jnp.float32)
    positions = first_row - extra + jnp.arange(row_count + extra, dtype=jnp.int32)
    all_ages = token_ages(positions, user_starts)
    out_rows = row_count + reach * (layer_count - 1)
    normed = rms_norm(hidden, norm_gains[0, 0]).astype(jnp.bfloat16)
    hidden = hidden[-out_rows:] + convolve(normed, tap_tables[0], all_ages[-out_rows:], out_rows)
    hidden = feed_forward(hidden, norm_gains[0, 1], gate_weight[0], up_weight[0], down_weight[0])
    return hidden.astype(jnp.bfloat16)


def solution(mesh):
    return jax.shard_map(
        body,
        mesh=mesh,
        in_specs=(
            P(("row", "col")),
            P(),
            P(("row", "col"), None),
            P(),
            P(),
            P(),
            P(None, "col", None),
            P(None, "col", None),
            P(None, "col", None),
        ),
        out_specs=P(("row", "col"), None),
        check_vma=False,
    )
```

profile of v0, /device:TPU:2, one launch (start us, length us, event | category | flops | bytes accessed | tf_op | source)
XLA Modules:
  0.0 230.7 jit_solution(10582264455192001664)
XLA Ops:
  8.1 3.4 %collective-permute-start = (s32[256]{0:T(256)}, s32[256]{0:T(256)S(1)}, u32[]{:S(2)}, u32[]{:S(2)}) collective-permute-start(s32[256]{0:T(256)} %param.11), channel_id=1, source_target_pairs={{0,1},{1,2},{2,3},{3,4},{4,5},{5,6},{6,7},{7,8},{8,9},{9,10},{10,1... | collective-permute-start | bytes 3080 | tf_op jit(solution)/shard_map/ppermute | solution.py:13
  13.9 2.2 select_bitcast_fusion
  16.1 69.4 %all-gather.3 = bf16[32,2,1024]{2,1,0:T(2,128)(2,1)S(1)} all-gather(bf16[1,2,1024]{2,1,0:T(2,128)(2,1)S(1)} %bitcast.163), channel_id=1, replica_groups=mesh['row'=4,'col'=8] {'row','col'}, dimensions={0}, use_global_device_ids=true | all-gather | bytes 135168 | tf_op jit(solution)/shard_map/all_gather | solution.py:90
  85.9 2.1 gather_fusion
  88.8 124.7 %while.17 = (s32[]{:T(128)}, f32[256,1024]{1,0:T(8,128)S(1)}, s32[256]{0:T(256)S(1)}, bf16[511,1024]{1,0:T(8,128)(2,1)S(1)}, f32[256,1024]{1,0:T(8,128)}, /*inde...) while((s32[]{:T(128)}, f32[256,1024]{1,0:T(8,128)S(1)}, ...), condition=%wide.region_4.5_spmd.clone, body=%wide.region_3.4_spmd.clone.sunk | while | flops 33825024 | bytes 19289948 | solution.py:50
  88.9 1.5 constant_dynamic-slice_fusion.35
  90.5 1.4 constant_dynamic-slice_fusion.34
  92.3 12.3 %select_add_fusion.3 = f32[256,1024]{1,0:T(8,128)S(1)} fusion(f32[256,1024]{1,0:T(8,128)S(1)} %get-tuple-element.605, f32[1024]{0:T(1024)S(1)} %bitcast.128, bf16[511,1024]{1,0:T(8,128)(2,1)S(1)} %get-tuple-element.679, s32[]{:T(128)S(6)} %select_n.1373, f32[1024]{0:T(1024)S(1)} %bitcast.129, s32[]{:T(128)S(6)} %select_n.1374, ...), kind=kLoop, calls=%fused_computation.26.clone.1 | loop fusion | flops 33816576 | bytes 19013760 | tf_op jit(solution)/shard_map/while/body/eval_jaxpr/add | solution.py:46
  104.7 1.2 constant_dynamic-slice_fusion.35
  106.1 1.4 constant_dynamic-slice_fusion.34
  107.8 12.3 %select_add_fusion.3 = f32[256,1024]{1,0:T(8,128)S(1)} fusion(f32[256,1024]{1,0:T(8,128)S(1)} %get-tuple-element.605, f32[1024]{0:T(1024)S(1)} %bitcast.128, bf16[511,1024]{1,0:T(8,128)(2,1)S(1)} %get-tuple-element.679, s32[]{:T(128)S(6)} %select_n.1373, f32[1024]{0:T(1024)S(1)} %bitcast.129, s32[]{:T(128)S(6)} %select_n.1374, ...), kind=kLoop, calls=%fused_computation.26.clone.1 | loop fusion | flops 33816576 | bytes 19013760 | tf_op jit(solution)/shard_map/while/body/eval_jaxpr/add | solution.py:46
  120.3 1.2 constant_dynamic-slice_fusion.35
  121.6 1.4 constant_dynamic-slice_fusion.34
  123.4 12.3 %select_add_fusion.3 = f32[256,1024]{1,0:T(8,128)S(1)} fusion(f32[256,1024]{1,0:T(8,128)S(1)} %get-tuple-element.605, f32[1024]{0:T(1024)S(1)} %bitcast.128, bf16[511,1024]{1,0:T(8,128)(2,1)S(1)} %get-tuple-element.679, s32[]{:T(128)S(6)} %select_n.1373, f32[1024]{0:T(1024)S(1)} %bitcast.129, s32[]{:T(128)S(6)} %select_n.1374, ...), kind=kLoop, calls=%fused_computation.26.clone.1 | loop fusion | flops 33816576 | bytes 19013760 | tf_op jit(solution)/shard_map/while/body/eval_jaxpr/add | solution.py:46
  135.8 1.2 constant_dynamic-slice_fusion.35
  137.2 1.4 constant_dynamic-slice_fusion.34
  138.9 12.3 %select_add_fusion.3 = f32[256,1024]{1,0:T(8,128)S(1)} fusion(f32[256,1024]{1,0:T(8,128)S(1)} %get-tuple-element.605, f32[1024]{0:T(1024)S(1)} %bitcast.128, bf16[511,1024]{1,0:T(8,128)(2,1)S(1)} %get-tuple-element.679, s32[]{:T(128)S(6)} %select_n.1373, f32[1024]{0:T(1024)S(1)} %bitcast.129, s32[]{:T(128)S(6)} %select_n.1374, ...), kind=kLoop, calls=%fused_computation.26.clone.1 | loop fusion | flops 33816576 | bytes 19013760 | tf_op jit(solution)/shard_map/while/body/eval_jaxpr/add | solution.py:46
  151.4 1.2 constant_dynamic-slice_fusion.35
  152.7 1.4 constant_dynamic-slice_fusion.34
  154.5 12.3 %select_add_fusion.3 = f32[256,1024]{1,0:T(8,128)S(1)} fusion(f32[256,1024]{1,0:T(8,128)S(1)} %get-tuple-element.605, f32[1024]{0:T(1024)S(1)} %bitcast.128, bf16[511,1024]{1,0:T(8,128)(2,1)S(1)} %get-tuple-element.679, s32[]{:T(128)S(6)} %select_n.1373, f32[1024]{0:T(1024)S(1)} %bitcast.129, s32[]{:T(128)S(6)} %select_n.1374, ...), kind=kLoop, calls=%fused_computation.26.clone.1 | loop fusion | flops 33816576 | bytes 19013760 | tf_op jit(solution)/shard_map/while/body/eval_jaxpr/add | solution.py:46
  166.9 1.2 constant_dynamic-slice_fusion.35
  168.3 1.4 constant_dynamic-slice_fusion.34
  170.0 12.3 %select_add_fusion.3 = f32[256,1024]{1,0:T(8,128)S(1)} fusion(f32[256,1024]{1,0:T(8,128)S(1)} %get-tuple-element.605, f32[1024]{0:T(1024)S(1)} %bitcast.128, bf16[511,1024]{1,0:T(8,128)(2,1)S(1)} %get-tuple-element.679, s32[]{:T(128)S(6)} %select_n.1373, f32[1024]{0:T(1024)S(1)} %bitcast.129, s32[]{:T(128)S(6)} %select_n.1374, ...), kind=kLoop, calls=%fused_computation.26.clone.1 | loop fusion | flops 33816576 | bytes 19013760 | tf_op jit(solution)/shard_map/while/body/eval_jaxpr/add | solution.py:46
  182.5 1.2 constant_dynamic-slice_fusion.35
  183.8 1.4 constant_dynamic-slice_fusion.34
  185.6 12.3 %select_add_fusion.3 = f32[256,1024]{1,0:T(8,128)S(1)} fusion(f32[256,1024]{1,0:T(8,128)S(1)} %get-tuple-element.605, f32[1024]{0:T(1024)S(1)} %bitcast.128, bf16[511,1024]{1,0:T(8,128)(2,1)S(1)} %get-tuple-element.679, s32[]{:T(128)S(6)} %select_n.1373, f32[1024]{0:T(1024)S(1)} %bitcast.129, s32[]{:T(128)S(6)} %select_n.1374, ...), kind=kLoop, calls=%fused_computation.26.clone.1 | loop fusion | flops 33816576 | bytes 19013760 | tf_op jit(solution)/shard_map/while/body/eval_jaxpr/add | solution.py:46
  198.0 1.2 constant_dynamic-slice_fusion.35
  199.4 1.4 constant_dynamic-slice_fusion.34
  201.2 12.3 %select_add_fusion.3 = f32[256,1024]{1,0:T(8,128)S(1)} fusion(f32[256,1024]{1,0:T(8,128)S(1)} %get-tuple-element.605, f32[1024]{0:T(1024)S(1)} %bitcast.128, bf16[511,1024]{1,0:T(8,128)(2,1)S(1)} %get-tuple-element.679, s32[]{:T(128)S(6)} %select_n.1373, f32[1024]{0:T(1024)S(1)} %bitcast.129, s32[]{:T(128)S(6)} %select_n.1374, ...), kind=kLoop, calls=%fused_computation.26.clone.1 | loop fusion | flops 33816576 | bytes 19013760 | tf_op jit(solution)/shard_map/while/body/eval_jaxpr/add | solution.py:46
  213.7 1.3 copy-done
  215.4 3.9 %fusion.28 = f32[256,1024]{1,0:T(8,128)} fusion(bf16[1,1024,1024]{2,1,0:T(8,128)(2,1)} %all-gather.8.cloned.1.call-done, f32[1024]{0:T(1024)S(1)} %bitcast.165, f32[256]{0:T(256)S(1)} %add_rsqrt_fusion.1, f32[256,1024]{1,0:T(8,128)S(1)} %get-tuple-element.276, f32[511,1024]{1,0:T(8,128)} %copy-done), kind=kOutput, calls=%fused_computation.95 | convolution fusion | flops 537919488 | bytes 5248000 | tf_op jit(solution)/shard_map/dot_general | solution.py:56
  219.3 4.9 %fusion.36 = bf16[256,1024]{1,0:T(8,128)(2,1)} fusion(bf16[1,1024,1024]{2,1,0:T(8,128)(2,1)} %all-gather.12.cloned.1.call-done, bf16[1,1024,1024]{2,1,0:T(8,128)(2,1)} %all-gather.10.cloned.1.call-done, f32[256,1024]{1,0:T(8,128)} %fusion.28, f32[1024]{0:T(1024)S(1)} %bitcast.166, f32[256]{0:T(256)S(1)} %add_rsqrt_fusion.1, ...), kind=kOutput, calls=%fused_computation.101 | convolution fusion | flops 1077149696 | bytes 9966592 | tf_op jit(solution)/shard_map/dot_general | solution.py:68
  (52 shorter events, 6.1 us)
Async XLA Ops:
  6.5 79.2 %copy-start.3 = (s32[256]{0:T(256)S(1)}, s32[256]{0:T(256)}, u32[]{:S(2)}) copy-start(s32[256]{0:T(256)} %param.11) | copy-start | bytes 3076
  6.5 9.6 %copy-start.2 = (bf16[2,1024]{1,0:T(2,128)(2,1)S(1)}, bf16[2,1024]{1,0:T(2,128)(2,1)}, u32[]{:S(2)}) copy-start(bf16[2,1024]{1,0:T(2,128)(2,1)} %param.13) | copy-start | bytes 12292
  6.5 208.8 %all-gather.8.cloned.1.call-start = ((), (), s32[]{:S(2)}) async-start(), calls=%async_computation | async-start | bytes 2359296 | tf_op jit(solution)/shard_map/all_gather | solution.py:58
  7.3 212.0 %all-gather.10.cloned.1.call-start = ((), (), s32[]{:S(2)}) async-start(), calls=%async_computation.1 | async-start | bytes 2359296 | tf_op jit(solution)/shard_map/all_gather | solution.py:63
  8.0 211.3 %all-gather.12.cloned.1.call-start = ((), (), s32[]{:S(2)}) async-start(), calls=%async_computation.2 | async-start | bytes 2359296 | tf_op jit(solution)/shard_map/all_gather | solution.py:70
  8.1 77.6 %collective-permute-start = (s32[256]{0:T(256)}, s32[256]{0:T(256)S(1)}, u32[]{:S(2)}, u32[]{:S(2)}) collective-permute-start(s32[256]{0:T(256)} %param.11), channel_id=1, source_target_pairs={{0,1},{1,2},{2,3},{3,4},{4,5},{5,6},{6,7},{7,8},{8,9},{9,10},{10,1... | collective-permute-start | bytes 3080 | tf_op jit(solution)/shard_map/ppermute | solution.py:13
  213.7 1.4 copy-start
  215.4 3.9 %copy-start.1 = (f32[511,1024]{1,0:T(8,128)S(1)}, f32[511,1024]{1,0:T(8,128)}, u32[]{:S(2)}) copy-start(f32[511,1024]{1,0:T(8,128)} %copy-done) | copy-start | bytes 6279172
Sparse Core Ops, SparseCore 0:
  9.5 50.3 all-gather.7
  62.0 48.4 all-gather.9
  112.6 47.6 all-gather.11
where the time goes:
time: 233 us; the launch traced here: 231 us
  other arithmetic  104 us (45%)
  blocking collectives  69.4 us (30%)
  local copies, waits for them, and re-layouts  25.8 us (11%)
  between operations  13.2 us (6%)
  matrix products  8.77 us (4%)
  loops' own time  4.23 us (2%)
  starting transfers between devices  3.51 us (2%)
    add x8, other arithmetic, one_group(): accumulated = accumulated + jnp.where(keep, shifted * weights, 0.0)  98.5 us
    all_gather x1, blocking collectives, body(): lax.all_gather(catalogue, ('row', 'col'), axis=0, tiled=True)  69.4 us
    dynamic_slice x16, local copies, waits for them, and re-layouts, one_group(): weights = lax.dynamic_slice_in_dim(tap_table, lag_index, 1, 0)  21.4 us
    dot_general x1, matrix products, feed_forward(): jnp.dot(columns, lax.all_gather(down_rows, 'col', axis=0, tiled=True), pr...  4.87 us
  transfers between devices with their start and end apart: 4, of which 0 were waited for; matrix products, arithmetic and copies ran while one was open for 57% of the time, Pallas kernels for 0%

commit v1 on v0

--- a/solution.py
+++ b/solution.py
@@ -5,6 +5,18 @@
 
 epsilon = 1e-06
 group_taps = 32
+
+
+def doubled_up(x, axis, dim):
+    ways, here = (lax.axis_size(axis), lax.axis_index(axis))
+    grown, reach = (x, 1)
+    while reach < ways:
+        theirs = lax.ppermute(grown, axis, [(d, d ^ reach) for d in range(ways)])
+        mine_first = jnp.concatenate([grown, theirs], axis=dim)
+        theirs_first = jnp.concatenate([theirs, grown], axis=dim)
+        grown = jnp.where(here & reach == 0, mine_first, theirs_first)
+        reach = 2 * reach
+    return grown
 
 
 def from_behind(block, axis, distance):
@@ -87,7 +99,7 @@
     row_count = item_ids.shape[0]
     reach = conv_taps.shape[1] - 1
     layer_count = conv_taps.shape[0]
-    catalogue_all = lax.all_gather(catalogue, ("row", "col"), axis=0, tiled=True)
+    catalogue_all = doubled_up(catalogue, ("row", "col"), 0)
     device_index = lax.axis_index("row") * lax.axis_size("col") + lax.axis_index("col")
     first_row = device_index * row_count
     user_starts = jnp.cumsum(user_lengths) - user_lengths

time: 233 us -> 181 us (0.78)
  blocking collectives: 69.4 us -> 0 us
  waiting for transfers between devices: 1.45 us -> 10.5 us
  starting transfers between devices: 3.51 us -> 9.03 us
    all_gather x1 -> x0, blocking collectives: 69.4 us -> none  [body(): lax.all_gather(catalogue, ('row', 'col'), axis=0, tiled=True)]
    ppermute x0 -> x5, waiting for transfers between devices: none -> 9.07 us  [doubled_up(): theirs = lax.ppermute(grown, axis, [(d, d ^ reach) for d in range(ways)])]
    ppermute x0 -> x5, starting transfers between devices: none -> 6.55 us  [doubled_up(): theirs = lax.ppermute(grown, axis, [(d, d ^ reach) for d in range(ways)])]
  transfers between devices with their start and end apart: 4 -> 9, of which waited for: 0 -> 4; matrix products, arithmetic and copies ran while one was open for 57% -> 76% of each run, Pallas kernels for 0% -> 0%
where the time goes in v1:
time: 181 us; the launch traced here: 178 us
  other arithmetic  104 us (57%)
  local copies, waits for them, and re-layouts  27.7 us (15%)
  between operations  13.3 us (7%)
  waiting for transfers between devices  10.5 us (6%)
  starting transfers between devices  9.03 us (5%)
  matrix products  8.78 us (5%)
  loops' own time  4.24 us (2%)
    add x8, other arithmetic, one_group(): accumulated = accumulated + jnp.where(keep, shifted * weights, 0.0)  98.5 us
    dynamic_slice x16, local copies, waits for them, and re-layouts, one_group(): weights = lax.dynamic_slice_in_dim(tap_table, lag_index, 1, 0)  23.3 us
    ppermute x5, waiting for transfers between devices, doubled_up(): theirs = lax.ppermute(grown, axis, [(d, d ^ reach) for d in range(ways)])  9.07 us
    ppermute x5, starting transfers between devices, doubled_up(): theirs = lax.ppermute(grown, axis, [(d, d ^ reach) for d in range(ways)])  6.55 us
    dot_general x1, matrix products, feed_forward(): jnp.dot(columns, lax.all_gather(down_rows, 'col', axis=0, tiled=True), pr...  4.88 us
    another operation x1, loops' own time, convolve(): return lax.fori_loop(0, groups, one_group, blank)  4.24 us
    dot_general x1, matrix products, feed_forward(): jnp.dot(columns, lax.all_gather(gate_rows, 'col', axis=0, tiled=True), pr...  3.9 us
  transfers between devices with their start and end apart: 9, of which 4 were waited for; matrix products, arithmetic and copies ran while one was open for 76% of the time, Pallas kernels for 0%

profile of v1, /device:TPU:2, one launch (start us, length us, event | category | flops | bytes accessed | tf_op | source)
XLA Modules:
  0.0 177.9 jit_solution(8969971401221011926)
XLA Ops:
  8.1 1.6 collective-permute-start.1
  9.6 2.4 %collective-permute-start = (s32[256]{0:T(256)}, s32[256]{0:T(256)S(1)}, u32[]{:S(2)}, u32[]{:S(2)}) collective-permute-start(s32[256]{0:T(256)} %param.11), channel_id=1, source_target_pairs={{0,1},{1,2},{2,3},{3,4},{4,5},{5,6},{6,7},{7,8},{8,9},{9,10},{10,1... | collective-permute-start | bytes 3080 | tf_op jit(solution)/shard_map/ppermute | solution.py:25
  14.4 2.2 %select_bitcast_fusion = f32[256,1024]{1,0:T(8,128)} fusion(bf16[1,256,1024]{2,1,0:T(8,128)(2,1)} %param.15, s32[1024]{0:T(1024)} %bitcast.161), kind=kLoop, calls=%fused_computation.106 | loop fusion | flops 786432 | bytes 1576960 | tf_op jit(solution)/shard_map/squeeze | solution.py:117
  16.7 1.6 collective-permute-start.2
  18.5 1.9 %collective-permute-done.2 = bf16[4,1024]{1,0:T(4,128)(2,1)S(1)} collective-permute-done((bf16[4,1024]{1,0:T(4,128)(2,1)S(1)}, bf16[4,1024]{1,0:T(4,128)(2,1)S(1)}, u32[]{:S(2)}, u32[]{:S(2)}) %collective-permute-start.2) | collective-permute-done | bytes 8224 | tf_op jit(solution)/shard_map/ppermute | solution.py:14
  20.5 2.7 %collective-permute-start.3 = (bf16[8,1024]{1,0:T(8,128)(2,1)S(1)}, bf16[8,1024]{1,0:T(8,128)(2,1)S(1)}, u32[]{:S(2)}, u32[]{:S(2)}) collective-permute-start(bf16[8,1024]{1,0:T(8,128)(2,1)S(1)} %maximum_select_fusion.3), channel_id=1, source_target_pairs={{0,4},{1,5},{2,6},{3,7},{4,0},{5,1},{6,2},{7,3},{8,12},{9,13},{10,... | collective-permute-start | bytes 49160 | tf_op jit(solution)/shard_map/ppermute | solution.py:14
  23.2 2.3 %collective-permute-done.3 = bf16[8,1024]{1,0:T(8,128)(2,1)S(1)} collective-permute-done((bf16[8,1024]{1,0:T(8,128)(2,1)S(1)}, bf16[8,1024]{1,0:T(8,128)(2,1)S(1)}, u32[]{:S(2)}, u32[]{:S(2)}) %collective-permute-start.3) | collective-permute-done | bytes 16416 | tf_op jit(solution)/shard_map/ppermute | solution.py:14
  27.5 3.6 %collective-permute-done.5 = bf16[32,1024]{1,0:T(8,128)(2,1)S(1)} collective-permute-done((bf16[32,1024]{1,0:T(8,128)(2,1)S(1)}, bf16[32,1024]{1,0:T(8,128)(2,1)S(1)}, u32[]{:S(2)}, u32[]{:S(2)}) %collective-permute-start.5) | collective-permute-done | bytes 65568 | tf_op jit(solution)/shard_map/ppermute | solution.py:14
  31.2 2.1 %gather_fusion = bf16[511,1024]{1,0:T(8,128)(2,1)S(1)} fusion(bf16[64,1024]{1,0:T(8,128)(2,1)S(1)} %maximum_select_fusion, s32[1024]{0:T(1024)S(1)} %pad_clamp_fusion), kind=kCustom, calls=%fused_computation | custom fusion | bytes 2095100 | tf_op jit(solution)/shard_map/jit(_take)/gather | solution.py:112
  34.1 126.6 %while.17 = (s32[]{:T(128)}, f32[256,1024]{1,0:T(8,128)S(1)}, s32[256]{0:T(256)S(1)}, bf16[511,1024]{1,0:T(8,128)(2,1)S(1)}, f32[256,1024]{1,0:T(8,128)}, /*inde...) while((s32[]{:T(128)}, f32[256,1024]{1,0:T(8,128)S(1)}, ...), condition=%wide.region_4.5_spmd.clone, body=%wide.region_3.4_spmd.clone.sunk | while | flops 33825024 | bytes 19289948 | solution.py:62
  34.2 1.4 constant_dynamic-slice_fusion.35
  35.7 1.6 constant_dynamic-slice_fusion.34
  37.7 12.3 %select_add_fusion.3 = f32[256,1024]{1,0:T(8,128)S(1)} fusion(f32[256,1024]{1,0:T(8,128)S(1)} %get-tuple-element.605, f32[1024]{0:T(1024)S(1)} %bitcast.127, bf16[511,1024]{1,0:T(8,128)(2,1)S(1)} %get-tuple-element.679, s32[]{:T(128)S(6)} %select_n.1433, f32[1024]{0:T(1024)S(1)} %bitcast.128, s32[]{:T(128)S(6)} %select_n.1434, ...), kind=kLoop, calls=%fused_computation.26.clone.1 | loop fusion | flops 33816576 | bytes 19013760 | tf_op jit(solution)/shard_map/while/body/eval_jaxpr/add | solution.py:58
  50.1 1.5 constant_dynamic-slice_fusion.35
  51.7 1.6 constant_dynamic-slice_fusion.34
  53.7 12.3 %select_add_fusion.3 = f32[256,1024]{1,0:T(8,128)S(1)} fusion(f32[256,1024]{1,0:T(8,128)S(1)} %get-tuple-element.605, f32[1024]{0:T(1024)S(1)} %bitcast.127, bf16[511,1024]{1,0:T(8,128)(2,1)S(1)} %get-tuple-element.679, s32[]{:T(128)S(6)} %select_n.1433, f32[1024]{0:T(1024)S(1)} %bitcast.128, s32[]{:T(128)S(6)} %select_n.1434, ...), kind=kLoop, calls=%fused_computation.26.clone.1 | loop fusion | flops 33816576 | bytes 19013760 | tf_op jit(solution)/shard_map/while/body/eval_jaxpr/add | solution.py:58
  67.5 1.7 constant_dynamic-slice_fusion.34
  69.5 12.3 %select_add_fusion.3 = f32[256,1024]{1,0:T(8,128)S(1)} fusion(f32[256,1024]{1,0:T(8,128)S(1)} %get-tuple-element.605, f32[1024]{0:T(1024)S(1)} %bitcast.127, bf16[511,1024]{1,0:T(8,128)(2,1)S(1)} %get-tuple-element.679, s32[]{:T(128)S(6)} %select_n.1433, f32[1024]{0:T(1024)S(1)} %bitcast.128, s32[]{:T(128)S(6)} %select_n.1434, ...), kind=kLoop, calls=%fused_computation.26.clone.1 | loop fusion | flops 33816576 | bytes 19013760 | tf_op jit(solution)/shard_map/while/body/eval_jaxpr/add | solution.py:58
  82.0 1.5 constant_dynamic-slice_fusion.35
  85.3 12.3 %select_add_fusion.3 = f32[256,1024]{1,0:T(8,128)S(1)} fusion(f32[256,1024]{1,0:T(8,128)S(1)} %get-tuple-element.605, f32[1024]{0:T(1024)S(1)} %bitcast.127, bf16[511,1024]{1,0:T(8,128)(2,1)S(1)} %get-tuple-element.679, s32[]{:T(128)S(6)} %select_n.1433, f32[1024]{0:T(1024)S(1)} %bitcast.128, s32[]{:T(128)S(6)} %select_n.1434, ...), kind=kLoop, calls=%fused_computation.26.clone.1 | loop fusion | flops 33816576 | bytes 19013760 | tf_op jit(solution)/shard_map/while/body/eval_jaxpr/add | solution.py:58
  99.3 1.4 constant_dynamic-slice_fusion.34
  101.1 12.3 %select_add_fusion.3 = f32[256,1024]{1,0:T(8,128)S(1)} fusion(f32[256,1024]{1,0:T(8,128)S(1)} %get-tuple-element.605, f32[1024]{0:T(1024)S(1)} %bitcast.127, bf16[511,1024]{1,0:T(8,128)(2,1)S(1)} %get-tuple-element.679, s32[]{:T(128)S(6)} %select_n.1433, f32[1024]{0:T(1024)S(1)} %bitcast.128, s32[]{:T(128)S(6)} %select_n.1434, ...), kind=kLoop, calls=%fused_computation.26.clone.1 | loop fusion | flops 33816576 | bytes 19013760 | tf_op jit(solution)/shard_map/while/body/eval_jaxpr/add | solution.py:58
  113.5 1.5 constant_dynamic-slice_fusion.35
  115.1 1.4 constant_dynamic-slice_fusion.34
  116.9 12.3 %select_add_fusion.3 = f32[256,1024]{1,0:T(8,128)S(1)} fusion(f32[256,1024]{1,0:T(8,128)S(1)} %get-tuple-element.605, f32[1024]{0:T(1024)S(1)} %bitcast.127, bf16[511,1024]{1,0:T(8,128)(2,1)S(1)} %get-tuple-element.679, s32[]{:T(128)S(6)} %select_n.1433, f32[1024]{0:T(1024)S(1)} %bitcast.128, s32[]{:T(128)S(6)} %select_n.1434, ...), kind=kLoop, calls=%fused_computation.26.clone.1 | loop fusion | flops 33816576 | bytes 19013760 | tf_op jit(solution)/shard_map/while/body/eval_jaxpr/add | solution.py:58
  130.7 1.5 constant_dynamic-slice_fusion.34
  132.6 12.3 %select_add_fusion.3 = f32[256,1024]{1,0:T(8,128)S(1)} fusion(f32[256,1024]{1,0:T(8,128)S(1)} %get-tuple-element.605, f32[1024]{0:T(1024)S(1)} %bitcast.127, bf16[511,1024]{1,0:T(8,128)(2,1)S(1)} %get-tuple-element.679, s32[]{:T(128)S(6)} %select_n.1433, f32[1024]{0:T(1024)S(1)} %bitcast.128, s32[]{:T(128)S(6)} %select_n.1434, ...), kind=kLoop, calls=%fused_computation.26.clone.1 | loop fusion | flops 33816576 | bytes 19013760 | tf_op jit(solution)/shard_map/while/body/eval_jaxpr/add | solution.py:58
  145.0 1.5 constant_dynamic-slice_fusion.35
  146.6 1.4 constant_dynamic-slice_fusion.34
  148.4 12.3 %select_add_fusion.3 = f32[256,1024]{1,0:T(8,128)S(1)} fusion(f32[256,1024]{1,0:T(8,128)S(1)} %get-tuple-element.605, f32[1024]{0:T(1024)S(1)} %bitcast.127, bf16[511,1024]{1,0:T(8,128)(2,1)S(1)} %get-tuple-element.679, s32[]{:T(128)S(6)} %select_n.1433, f32[1024]{0:T(1024)S(1)} %bitcast.128, s32[]{:T(128)S(6)} %select_n.1434, ...), kind=kLoop, calls=%fused_computation.26.clone.1 | loop fusion | flops 33816576 | bytes 19013760 | tf_op jit(solution)/shard_map/while/body/eval_jaxpr/add | solution.py:58
  162.6 3.9 %fusion.28 = f32[256,1024]{1,0:T(8,128)} fusion(bf16[1,1024,1024]{2,1,0:T(8,128)(2,1)} %all-gather.7.cloned.1.call-done, f32[1024]{0:T(1024)S(1)} %bitcast.163, f32[256]{0:T(256)S(1)} %add_rsqrt_fusion.1, f32[256,1024]{1,0:T(8,128)S(1)} %get-tuple-element.276, f32[511,1024]{1,0:T(8,128)} %copy-done), kind=kOutput, calls=%fused_computation.95 | convolution fusion | flops 537919488 | bytes 5248000 | tf_op jit(solution)/shard_map/dot_general | solution.py:68
  166.5 4.9 %fusion.36 = bf16[256,1024]{1,0:T(8,128)(2,1)} fusion(bf16[1,1024,1024]{2,1,0:T(8,128)(2,1)} %all-gather.11.cloned.1.call-done, bf16[1,1024,1024]{2,1,0:T(8,128)(2,1)} %all-gather.9.cloned.1.call-done, f32[256,1024]{1,0:T(8,128)} %fusion.28, f32[1024]{0:T(1024)S(1)} %bitcast.164, f32[256]{0:T(256)S(1)} %add_rsqrt_fusion.1, ...), kind=kOutput, calls=%fused_computation.101 | convolution fusion | flops 1077149696 | bytes 9966592 | tf_op jit(solution)/shard_map/dot_general | solution.py:80
  (65 shorter events, 14.8 us)
Async XLA Ops:
  6.5 10.1 %copy-start.3 = (bf16[2,1024]{1,0:T(2,128)(2,1)S(1)}, bf16[2,1024]{1,0:T(2,128)(2,1)}, u32[]{:S(2)}) copy-start(bf16[2,1024]{1,0:T(2,128)(2,1)} %param.13) | copy-start | bytes 12292
  6.5 16.6 %copy-start.2 = (s32[256]{0:T(256)S(1)}, s32[256]{0:T(256)}, u32[]{:S(2)}) copy-start(s32[256]{0:T(256)} %param.11) | copy-start | bytes 3076
  6.5 156.0 %all-gather.7.cloned.1.call-start = ((), (), s32[]{:S(2)}) async-start(), calls=%async_computation | async-start | bytes 2359296 | tf_op jit(solution)/shard_map/all_gather | solution.py:70
  7.3 159.2 %all-gather.11.cloned.1.call-start = ((), (), s32[]{:S(2)}) async-start(), calls=%async_computation.2 | async-start | bytes 2359296 | tf_op jit(solution)/shard_map/all_gather | solution.py:82
  8.0 158.5 %all-gather.9.cloned.1.call-start = ((), (), s32[]{:S(2)}) async-start(), calls=%async_computation.1 | async-start | bytes 2359296 | tf_op jit(solution)/shard_map/all_gather | solution.py:75
  8.1 8.6 %collective-permute-start.1 = (bf16[2,1024]{1,0:T(2,128)(2,1)}, bf16[2,1024]{1,0:T(2,128)(2,1)S(1)}, u32[]{:S(2)}, u32[]{:S(2)}) collective-permute-start(bf16[2,1024]{1,0:T(2,128)(2,1)} %param.13), channel_id=1, source_target_pairs={{0,1},{1,0},{2,3},{3,2},{4,5},{5,4},{6,7},{7,6},{8,9},{9,8},{10,11... | collective-permute-start | bytes 12296 | tf_op jit(solution)/shard_map/ppermute | solution.py:14
  9.6 8.8 %collective-permute-start = (s32[256]{0:T(256)}, s32[256]{0:T(256)S(1)}, u32[]{:S(2)}, u32[]{:S(2)}) collective-permute-start(s32[256]{0:T(256)} %param.11), channel_id=1, source_target_pairs={{0,1},{1,2},{2,3},{3,4},{4,5},{5,6},{6,7},{7,8},{8,9},{9,10},{10,1... | collective-permute-start | bytes 3080 | tf_op jit(solution)/shard_map/ppermute | solution.py:25
  16.7 3.7 %collective-permute-start.2 = (bf16[4,1024]{1,0:T(4,128)(2,1)S(1)}, bf16[4,1024]{1,0:T(4,128)(2,1)S(1)}, u32[]{:S(2)}, u32[]{:S(2)}) collective-permute-start(bf16[4,1024]{1,0:T(4,128)(2,1)S(1)} %maximum_select_fusion.4), channel_id=1, source_target_pairs={{0,2},{1,3},{2,0},{3,1},{4,6},{5,7},{6,4},{7,5},{8,10},{9,11},{10,... | collective-permute-start | bytes 24584 | tf_op jit(solution)/shard_map/ppermute | solution.py:14
  20.5 5.1 %collective-permute-start.3 = (bf16[8,1024]{1,0:T(8,128)(2,1)S(1)}, bf16[8,1024]{1,0:T(8,128)(2,1)S(1)}, u32[]{:S(2)}, u32[]{:S(2)}) collective-permute-start(bf16[8,1024]{1,0:T(8,128)(2,1)S(1)} %maximum_select_fusion.3), channel_id=1, source_target_pairs={{0,4},{1,5},{2,6},{3,7},{4,0},{5,1},{6,2},{7,3},{8,12},{9,13},{10,... | collective-permute-start | bytes 49160 | tf_op jit(solution)/shard_map/ppermute | solution.py:14
  25.5 1.3 collective-permute-start.4
  26.8 4.3 %collective-permute-start.5 = (bf16[32,1024]{1,0:T(8,128)(2,1)S(1)}, bf16[32,1024]{1,0:T(8,128)(2,1)S(1)}, u32[]{:S(2)}, u32[]{:S(2)}) collective-permute-start(bf16[32,1024]{1,0:T(8,128)(2,1)S(1)} %maximum_select_fusion.1), channel_id=1, source_target_pairs={{0,16},{1,17},{2,18},{3,19},{4,20},{5,21},{6,22},{7,23},{8,24},{9,... | collective-permute-start | bytes 196616 | tf_op jit(solution)/shard_map/ppermute | solution.py:14
  160.9 1.3 copy-start
  162.5 3.9 %copy-start.1 = (f32[511,1024]{1,0:T(8,128)S(1)}, f32[511,1024]{1,0:T(8,128)}, u32[]{:S(2)}) copy-start(f32[511,1024]{1,0:T(8,128)} %copy-done) | copy-start | bytes 6279172
Sparse Core Ops, SparseCore 0:
  9.5 50.7 all-gather.6
  62.4 47.6 all-gather.10
  112.2 47.6 all-gather.8
